TPU v7x, 32 devices: a whole 2x2x4 slice. The times are simulated.
32 devices in a mesh: dom: 16 (over z, x, core), feat: 2 (over y).
Axes of the slice: x: 2, y: 2, z: 4, core: 2. Of those that a mesh axis runs over, the one named last changes fastest.
Arguments:
- features: bfloat16 [65536, 1024], P('dom', 'feat'), may hold values from -6 to 6
- w_self: bfloat16 [1024, 256], P('feat'), may hold values from -0.1875 to 0.1875
- w_neigh: bfloat16 [1024, 256], P('feat'), may hold values from -0.1875 to 0.1875
- hidden_bias: float32 [256], replicated, may hold values from -3 to 3
- edge_tiles: bfloat16 [16, 102, 128, 128], P('dom'), may hold values from 0 to 0.099609375
- tile_dst: int32 [16, 102], P('dom'), may hold values from 0 to 31, as said below
- tile_src: int32 [16, 102], P('dom'), may hold values from 0 to 47, as said below
- tile_count: int32 [16], P('dom'), may hold values from 12 to 102, as said below
- bound_rows: int32 [16, 256], P('dom'), may hold values from 0 to 4095, as said below
- send_pick: int32 [16, 16, 128], P('dom'), may hold values from 0 to 255, as said below
- cotangent: bfloat16 [65536, 256], P(('dom', 'feat')), may hold values from -0.0234375 to 0.0234375
Outputs:
- hidden: bfloat16 [65536, 256], P(('dom', 'feat'))
- grad_self: bfloat16 [1024, 256], P('feat')
- grad_neigh: bfloat16 [1024, 256], P('feat')
- grad_bias: float32 [256], replicated
Inputs may be any that keep to these rules, and one draw needn't show every extreme that they name: Within a partition the pairs (tile_dst, tile_src) of its 102 slots are distinct. `tile_src`: A source block below 32 is a row tile of the partition itself; block 32 + q is the block received from partition q. Slots from tile_count[p] on are unused. Some partition uses all 102 slots. `bound_rows`: distinct within each partition. Each list send_pick[p, q] has no repeats.
All inputs are finite; a program needn't handle non-finite values.
Results may differ from a plain program's by a relative error of at most 0.009.
The roundings to bfloat16 on the way count: a program that leaves them out, or rounds other values in their place, can miss the bound.
Values may be sent and summed in bfloat16 or wider, within the bound.
A program may use at most 128 MiB of HBM per device.

v0:
```python
import jax
import jax.numpy as jnp
from jax import lax
from jax.sharding import PartitionSpec as P

TILE = 128


def tile_sums(source, local_tiles, dest_list, source_list, live_count, dest_tiles):
    slice_width = source.shape[1]
    blocks = source.reshape(source.shape[0] // TILE, TILE, slice_width)
    picked = jnp.take(blocks, source_list, axis=0)
    products = jnp.einsum("etc,ecf->etf", local_tiles, picked, preferred_element_type=jnp.float32)
    slot_ids = jnp.arange(source_list.shape[0], dtype=jnp.int32)
    live_slots = (slot_ids < live_count).astype(jnp.float32)
    dest_ids = jnp.arange(dest_tiles, dtype=jnp.int32)[:, None]
    onehot = (dest_list[None, :] == dest_ids).astype(jnp.float32) * live_slots[None, :]
    summed = jnp.einsum("de,etf->dtf", onehot, products, precision=lax.Precision.HIGHEST)
    return summed.reshape(dest_tiles * TILE, slice_width).astype(jnp.bfloat16)


def body(
    features,
    w_self,
    w_neigh,
    hidden_bias,
    edge_tiles,
    tile_dst,
    tile_src,
    tile_count,
    bound_rows,
    send_pick,
    cotangent,
):
    part_count = lax.axis_size("dom")
    slice_width = features.shape[1]
    node_rows = features.shape[0]
    boundary = jnp.take(features, bound_rows[0], axis=0)
    everyone = lax.all_gather(boundary, "dom", axis=0, tiled=True)
    pick_lists = lax.all_to_all(send_pick, "dom", split_axis=1, concat_axis=0, tiled=True)
    offsets = (jnp.arange(part_count, dtype=jnp.int32) * boundary.shape[0])[:, None]
    wanted = (pick_lists[:, 0, :] + offsets).reshape(-1)
    received = jnp.take(everyone, wanted, axis=0)
    source = jnp.concatenate([features, received], 0)
    aggregated = tile_sums(
        source, edge_tiles[0], tile_dst[0], tile_src[0], tile_count[0], node_rows // TILE
    )
    stacked = jnp.concatenate([features, aggregated], 1)
    weights = jnp.concatenate([w_self, w_neigh], 0)
    row_block = stacked
    summed = lax.psum_scatter(
        jnp.dot(row_block, weights, preferred_element_type=jnp.float32),
        "feat",
        scatter_dimension=0,
        tiled=True,
    )
    preact = summed + hidden_bias
    hidden = jnp.maximum(preact, 0.0).astype(jnp.bfloat16)
    pre_grad = jnp.where(preact > 0.0, cotangent, jnp.zeros_like(cotangent))
    shard_rows = lax.all_gather(pre_grad, "feat", axis=0, tiled=True)
    row_block = stacked
    product = lax.dot_general(
        row_block, shard_rows, (((0,), (0,)), ((), ())), preferred_element_type=jnp.float32
    )
    all_grads = product
    bias_grad = jnp.sum(shard_rows.astype(jnp.float32), 0)
    all_grads, bias_grad = lax.psum((all_grads, bias_grad), "dom")
    grad_self = all_grads[:slice_width]
    grad_neigh = all_grads[slice_width:]
    return (hidden, grad_self.astype(jnp.bfloat16), grad_neigh.astype(jnp.bfloat16), bias_grad)


def solution(mesh):
    placed = (
        P("dom", "feat"),
        P("feat", None),
        P("feat", None),
        P(),
        P("dom", None, None, None),
        P("dom", None),
        P("dom", None),
        P("dom"),
        P("dom", None),
        P("dom", None, None),
        P(("dom", "feat"), None),
    )
    return jax.shard_map(
        body,
        mesh=mesh,
        in_specs=placed,
        out_specs=(P(("dom", "feat"), None), P("feat", None), P("feat", None), P()),
        check_vma=False,
    )
```

profile of v0, /device:TPU:0, one launch (start us, length us, event | category | flops | bytes accessed | tf_op | source)
XLA Modules:
  0.0 343.9 jit_solution(6246623295148714957)
XLA Ops:
  7.2 0.8 compare_select_fusion.3
  8.9 4.6 %gather_fusion = bf16[256,512]{1,0:T(8,128)(2,1)} fusion(bf16[4096,512]{1,0:T(8,128)(2,1)} %param.11, s32[1024]{0:T(1024)S(1)} %pad_clamp_fusion.1), kind=kCustom, calls=%fused_computation | custom fusion | bytes 525312 | tf_op jit(solution)/shard_map/jit(_take)/gather | solution.py:38
  13.5 1.8 broadcast_select_fusion.1
  15.3 7.4 %all-to-all-start = ((s32[1,16,128]{2,0,1:T(1,128)}), s32[1,16,128]{2,0,1:T(1,128)S(1)}, u32[]{:S(2)}, u32[]{:S(2)}) async-start(s32[1,16,128]{2,0,1:T(1,128)} %bitcast.45), calls=%async_computation | async-start | bytes 16384 | tf_op jit(solution)/shard_map/all_to_all | solution.py:40
  24.7 4.3 %all-to-all-done = s32[1,16,128]{2,0,1:T(1,128)S(1)} async-done(((s32[1,16,128]{2,0,1:T(1,128)}), s32[1,16,128]{2,0,1:T(1,128)S(1)}, u32[]{:S(2)}, u32[]{:S(2)}) %all-to-all-start) | async-done | bytes 8224 | tf_op jit(solution)/shard_map/all_to_all | solution.py:40
  29.2 39.3 %all-gather.3.cloned.1.call-done = bf16[4096,512]{1,0:T(8,128)(2,1)} async-done(((bf16[256,512]{1,0:T(8,128)(2,1)}), bf16[4096,512]{1,0:T(8,128)(2,1)}) %all-gather.3.cloned.1.call-update) | async-done | bytes 4194320 | tf_op jit(solution)/shard_map/all_gather | solution.py:39
  68.5 12.2 %gather_fusion.1 = bf16[2048,512]{1,0:T(8,128)(2,1)} fusion(bf16[4096,512]{1,0:T(8,128)(2,1)} %all-gather.3.cloned.1.call-done, s32[2048]{0:T(1024)S(1)} %broadcast_clamp_fusion), kind=kCustom, calls=%fused_computation.1 | custom fusion | bytes 4202496 | tf_op jit(solution)/shard_map/jit(_take)/gather | solution.py:43
  80.7 1.9 broadcast_select_fusion
  82.6 0.9 copy-done.2
  83.5 3.0 pad_maximum_fusion.1
  86.5 10.2 %gather_fusion.2 = bf16[102,128,512]{2,1,0:T(8,128)(2,1)} fusion(bf16[48,128,512]{2,1,0:T(8,128)(2,1)} %bitcast.39, s32[1024]{0:T(1024)S(1)} %pad_clamp_fusion), kind=kCustom, calls=%fused_computation.2 | custom fusion | bytes 26739096 | tf_op jit(solution)/shard_map/jit(_take)/gather | solution.py:12
  96.7 13.8 %fusion.3 = f32[102,128,512]{1,2,0:T(8,128)} fusion(bf16[102,128,512]{2,1,0:T(8,128)(2,1)} %gather_fusion.2, pred[102]{0:T(512)(128)(4,1)S(1)} %compare_and_fusion.2, bf16[1,102,128,128]{3,2,1,0:T(8,128)(2,1)S(1)} %copy-done), kind=kOutput, calls=%fused_computation.6 | convolution fusion | flops 1717960704 | bytes 43450472 | tf_op jit(solution)/shard_map/etc,ecf->etf/dot_general | solution.py:13
  110.5 28.4 %copy.21 = f32[102,128,512]{2,0,1:T(8,128)} copy(f32[102,128,512]{1,2,0:T(8,128)} %fusion.3) | data formatting | bytes 53477376 | tf_op jit(solution)/shard_map/etc,ecf->etf/dot_general | solution.py:13
  139.0 16.6 %convolution_convert_fusion = bf16[32,128,512]{2,0,1:T(8,128)(2,1)S(1)} fusion(f32[102,128,512]{2,0,1:T(8,128)} %copy.21, f32[102]{0:T(128)S(1)} %compare_convert_fusion, s32[102]{0:T(128)S(1)} %bitcast.48), kind=kOutput, calls=%fused_computation.14 | convolution fusion | flops 2569017856 | bytes 30933808 | tf_op jit(solution)/shard_map/de,etf->dtf/dot_general | solution.py:18
  155.6 2.4 copy.22
  158.0 2.0 copy-done.5
  159.9 3.9 %fusion.8 = f32[4096,256]{1,0:T(8,128)} fusion(bf16[4096,512]{1,0:T(8,128)(2,1)S(1)} %bitcast.40, bf16[4096,512]{1,0:T(8,128)(2,1)S(1)} %copy-done.3, bf16[512,256]{1,0:T(8,128)(2,1)S(1)} %copy-done.10, bf16[512,256]{1,0:T(8,128)(2,1)S(1)} %copy-done.11), kind=kOutput, calls=%fused_computation.11 | convolution fusion | flops 2165309440 | bytes 13107200 | tf_op jit(solution)/shard_map/dot_general | solution.py:52
  164.1 52.8 %reduce-scatter.2.cloned.1.call-done = f32[2048,256]{1,0:T(8,128)} async-done(((f32[4096,256]{1,0:T(8,128)}), f32[2048,256]{1,0:T(8,128)}) %reduce-scatter.2.cloned.1.call-update) | async-done | bytes 2097168 | tf_op jit(solution)/shard_map/reduce_scatter | solution.py:51
  216.9 3.0 compare_select_fusion
  220.0 1.2 maximum_convert_fusion
  221.2 32.1 %all-gather.5.cloned.1.call-done = bf16[4096,256]{1,0:T(8,128)(2,1)} async-done(((bf16[2048,256]{1,0:T(8,128)(2,1)}), bf16[4096,256]{1,0:T(8,128)(2,1)}) %all-gather.5.cloned.1.call-update) | async-done | bytes 2097168 | tf_op jit(solution)/shard_map/all_gather | solution.py:60
  253.3 7.6 %fusion.7 = f32[1024,256]{1,0:T(8,128)} fusion(bf16[4096,256]{1,0:T(8,128)(2,1)} %all-gather.5.cloned.1.call-done, bf16[4096,512]{1,0:T(8,128)(2,1)} %bitcast.41, bf16[4096,512]{1,0:T(8,128)(2,1)} %param.11), kind=kOutput, calls=%fused_computation.10 | convolution fusion | flops 2164260864 | bytes 11534336 | tf_op jit(solution)/shard_map/dot_general | solution.py:62
  261.4 74.1 %all-reduce.2 = (bf16[1024,256]{1,0:T(8,128)(2,1)}, f32[256]{0:T(256)}) all-reduce(f32[1024,256]{1,0:T(8,128)} %fusion.7, f32[256]{0:T(256)S(1)} %convert_reduce_fusion), channel_id=1, replica_groups=mesh['dom'=16,'feat'=2] {'dom'}, use_global_device_ids=true, to_apply=%region_1.2 | all-reduce | flops 262400 | bytes 1574912 | tf_op jit(solution)/shard_map/psum | solution.py:67
  335.5 1.9 fusion.23
  (40 shorter events, 3.3 us)
Async XLA Ops:
  7.2 89.6 %copy-start = (bf16[1,102,128,128]{3,2,1,0:T(8,128)(2,1)S(1)}, bf16[1,102,128,128]{3,2,1,0:T(8,128)(2,1)}, u32[]{:S(2)}) copy-start(bf16[1,102,128,128]{3,2,1,0:T(8,128)(2,1)} %param.15) | copy-start | bytes 10027012
  7.2 61.4 %all-gather.3.cloned.1.call-start = ((), (), s32[]{:S(2)}) async-start(), calls=%async_computation.2 | async-start | bytes 4456448 | tf_op jit(solution)/shard_map/all_gather | solution.py:39
  15.3 13.8 %all-to-all-start = ((s32[1,16,128]{2,0,1:T(1,128)}), s32[1,16,128]{2,0,1:T(1,128)S(1)}, u32[]{:S(2)}, u32[]{:S(2)}) async-start(s32[1,16,128]{2,0,1:T(1,128)} %bitcast.45), calls=%async_computation | async-start | bytes 16384 | tf_op jit(solution)/shard_map/all_to_all | solution.py:40
  22.7 194.2 %reduce-scatter.2.cloned.1.call-start = ((), (), s32[]{:S(2)}) async-start(), calls=%async_computation.3 | async-start | bytes 6291456 | tf_op jit(solution)/shard_map/reduce_scatter | solution.py:51
  80.7 2.8 copy-start.2
  110.5 28.4 %copy-start.9 = (s32[1,102]{1,0:T(1,128)S(1)}, s32[1,102]{1,0:T(1,128)}, u32[]{:S(2)}) copy-start(s32[1,102]{1,0:T(1,128)} %param.16) | copy-start | bytes 1228
  155.5 4.4 %copy-start.3 = (bf16[4096,512]{1,0:T(8,128)(2,1)S(1)}, bf16[4096,512]{1,0:T(8,128)(2,1)}, u32[]{:S(2)}) copy-start(bf16[4096,512]{1,0:T(8,128)(2,1)} %param.11) | copy-start | bytes 12582916
  155.5 4.4 %copy-start.10 = (bf16[512,256]{1,0:T(8,128)(2,1)S(1)}, bf16[512,256]{1,0:T(8,128)(2,1)}, u32[]{:S(2)}) copy-start(bf16[512,256]{1,0:T(8,128)(2,1)} %param.13) | copy-start | bytes 786436
  155.6 4.4 %copy-start.11 = (bf16[512,256]{1,0:T(8,128)(2,1)S(1)}, bf16[512,256]{1,0:T(8,128)(2,1)}, u32[]{:S(2)}) copy-start(bf16[512,256]{1,0:T(8,128)(2,1)} %param.12) | copy-start | bytes 786436
  158.0 2.0 copy-start.5
  163.8 53.1 %copy-start.7 = (bf16[2048,256]{1,0:T(8,128)(2,1)S(1)}, bf16[2048,256]{1,0:T(8,128)(2,1)}, u32[]{:S(2)}) copy-start(bf16[2048,256]{1,0:T(8,128)(2,1)} %param.21) | copy-start | bytes 3145732
  163.8 53.1 %copy-start.8 = (f32[256]{0:T(256)S(1)}, f32[256]{0:T(256)}, u32[]{:S(2)}) copy-start(f32[256]{0:T(256)} %param.14) | copy-start | bytes 3076
  163.8 89.4 %all-gather.5.cloned.1.call-start = ((), (), s32[]{:S(2)}) async-start(), calls=%async_computation.4 | async-start | bytes 3145728 | tf_op jit(solution)/shard_map/all_gather | solution.py:60
  216.9 3.1 copy-start.4
  253.3 7.6 %copy-start.6 = (bf16[4096,256]{1,0:T(8,128)(2,1)S(1)}, bf16[4096,256]{1,0:T(8,128)(2,1)}, u32[]{:S(2)}) copy-start(bf16[4096,256]{1,0:T(8,128)(2,1)} %all-gather.5.cloned.1.call-done) | copy-start | bytes 6291460
  253.3 84.1 %copy-start.1 = (bf16[1,102,128,128]{3,2,1,0:T(8,128)(2,1)S(1)}, bf16[1,102,128,128]{3,2,1,0:T(8,128)(2,1)}, u32[]{:S(2)}) copy-start(bf16[1,102,128,128]{3,2,1,0:T(8,128)(2,1)} %param.15) | copy-start | bytes 10027012
Sparse Core Ops, SparseCore 0:
  15.4 53.0 all-gather.2
  164.0 52.9 reduce-scatter.1
  220.1 33.1 all-gather.4
where the time goes:
time: 345 us; the launch traced here: 344 us
  waiting for transfers between devices  129 us (37%)
  blocking collectives  74.1 us (21%)
  local copies, waits for them, and re-layouts  62.7 us (18%)
  matrix products  41.8 us (12%)
  other arithmetic  14.5 us (4%)
  between operations  14.5 us (4%)
  starting transfers between devices  7.74 us (2%)
    psum x1, blocking collectives, body(): all_grads, bias_grad = lax.psum((all_grads, bias_grad), 'dom')  74.1 us
    reduce_scatter x1, waiting for transfers between devices, body(): lax.psum_scatter(jnp.dot(row_block, weights, preferred_element_type=jnp.f...  52.8 us
    all_gather x1, waiting for transfers between devices, body(): everyone = lax.all_gather(boundary, 'dom', axis=0, tiled=True)  39.3 us
    all_gather x1, waiting for transfers between devices, body(): shard_rows = lax.all_gather(pre_grad, 'feat', axis=0, tiled=True)  32.1 us
    dot_general x1, local copies, waits for them, and re-layouts, tile_sums(): jnp.einsum('etc,ecf->etf', local_tiles, picked, preferred_element_type=jn...  28.4 us
    dot_general x1, matrix products, tile_sums(): jnp.einsum('de,etf->dtf', onehot, products, precision=lax.Precision.HIGHEST)  16.6 us
    dot_general x1, matrix products, tile_sums(): jnp.einsum('etc,ecf->etf', local_tiles, picked, preferred_element_type=jn...  13.8 us
    gather x1, local copies, waits for them, and re-layouts, body(): received = jnp.take(everyone, wanted, axis=0)  12.2 us
  transfers between devices with their start and end apart: 4, of which 4 were waited for; matrix products, arithmetic and copies ran while one was open for 1% of the time, Pallas kernels for 0%

commit v1 on v0

--- a/solution.py
+++ b/solution.py
@@ -36,7 +36,8 @@
     slice_width = features.shape[1]
     node_rows = features.shape[0]
     boundary = jnp.take(features, bound_rows[0], axis=0)
-    everyone = lax.all_gather(boundary, "dom", axis=0, tiled=True)
+    repeated = jnp.stack([boundary] * lax.axis_size("dom"))
+    everyone = jnp.concatenate(lax.all_to_all(repeated, "dom", 0, 0), axis=0)
     pick_lists = lax.all_to_all(send_pick, "dom", split_axis=1, concat_axis=0, tiled=True)
     offsets = (jnp.arange(part_count, dtype=jnp.int32) * boundary.shape[0])[:, None]
     wanted = (pick_lists[:, 0, :] + offsets).reshape(-1)

time: 345 us -> 403 us (1.17)
  waiting for transfers between devices: 129 us -> 178 us
  starting transfers between devices: 7.74 us -> 14.2 us
    all_to_all x0 -> x1, waiting for transfers between devices: none -> 76.6 us  [body(): everyone = jnp.concatenate(lax.all_to_all(repeated, 'dom', 0, 0), axis=0)]
    all_gather x1 -> x0, waiting for transfers between devices: 39.3 us -> none  [body(): everyone = lax.all_gather(boundary, 'dom', axis=0, tiled=True)]
    reduce_scatter x1, waiting for transfers between devices: 52.8 us -> 69.3 us  [body(): lax.psum_scatter(jnp.dot(row_block, weights, preferred_element_type=jnp.f...]
    all_to_all x0 -> x1, starting transfers between devices: none -> 6.19 us  [body(): everyone = jnp.concatenate(lax.all_to_all(repeated, 'dom', 0, 0), axis=0)]
    all_to_all x1, waiting for transfers between devices: 4.32 us -> 0.01 us  [body(): lax.all_to_all(send_pick, 'dom', split_axis=1, concat_axis=0, tiled=True)]
  transfers between devices with their start and end apart: 4 -> 4, of which waited for: 4 -> 3; matrix products, arithmetic and copies ran while one was open for 1% -> 2% of each run, Pallas kernels for 0% -> 0%
where the time goes in v1:
time: 403 us; the launch traced here: 402 us
  waiting for transfers between devices  178 us (44%)
  blocking collectives  74.1 us (18%)
  local copies, waits for them, and re-layouts  66 us (16%)
  matrix products  41.8 us (10%)
  between operations  14.8 us (4%)
  starting transfers between devices  14.2 us (4%)
  other arithmetic  12.9 us (3%)
    all_to_all x1, waiting for transfers between devices, body(): everyone = jnp.concatenate(lax.all_to_all(repeated, 'dom', 0, 0), axis=0)  76.6 us
    psum x1, blocking collectives, body(): all_grads, bias_grad = lax.psum((all_grads, bias_grad), 'dom')  74.1 us
    reduce_scatter x1, waiting for transfers between devices, body(): lax.psum_scatter(jnp.dot(row_block, weights, preferred_element_type=jnp.f...  69.3 us
    all_gather x1, waiting for transfers between devices, body(): shard_rows = lax.all_gather(pre_grad, 'feat', axis=0, tiled=True)  32.1 us
    dot_general x1, local copies, waits for them, and re-layouts, tile_sums(): jnp.einsum('etc,ecf->etf', local_tiles, picked, preferred_element_type=jn...  28.4 us
    dot_general x1, matrix products, tile_sums(): jnp.einsum('de,etf->dtf', onehot, products, precision=lax.Precision.HIGHEST)  16.6 us
    dot_general x1, matrix products, tile_sums(): jnp.einsum('etc,ecf->etf', local_tiles, picked, preferred_element_type=jn...  13.8 us
    gather x1, local copies, waits for them, and re-layouts, body(): received = jnp.take(everyone, wanted, axis=0)  12.2 us
  transfers between devices with their start and end apart: 4, of which 3 were waited for; matrix products, arithmetic and copies ran while one was open for 2% of the time, Pallas kernels for 0%

profile of v1, /device:TPU:0, one launch (start us, length us, event | category | flops | bytes accessed | tf_op | source)
XLA Modules:
  0.0 401.9 jit_solution(10324330588477116181)
XLA Ops:
  7.2 7.7 %all-to-all-start = ((s32[1,16,128]{2,0,1:T(1,128)}), s32[1,16,128]{2,0,1:T(1,128)S(1)}, u32[]{:S(2)}, u32[]{:S(2)}) async-start(s32[1,16,128]{2,0,1:T(1,128)} %bitcast.46), calls=%async_computation | async-start | bytes 16384 | tf_op jit(solution)/shard_map/all_to_all | solution.py:41
  16.2 4.6 %gather_fusion = bf16[256,512]{1,0:T(8,128)(2,1)} fusion(bf16[4096,512]{1,0:T(8,128)(2,1)} %param.11, s32[1024]{0:T(1024)S(1)} %pad_clamp_fusion.1), kind=kCustom, calls=%fused_computation | custom fusion | bytes 525312 | tf_op jit(solution)/shard_map/jit(_take)/gather | solution.py:38
  20.9 1.8 broadcast_select_fusion.1
  22.6 3.3 stack.2
  26.0 6.2 %all-to-all-start.1 = ((bf16[16,256,512]{2,1,0:T(8,128)(2,1)}), bf16[16,256,512]{2,1,0:T(8,128)(2,1)}, u32[]{:S(2)}, u32[]{:S(2)}) async-start(bf16[16,256,512]{2,1,0:T(8,128)(2,1)} %stack.2), calls=%async_computation.1 | async-start | bytes 8388608 | tf_op jit(solution)/shard_map/all_to_all | solution.py:40
  33.1 76.6 %all-to-all-done.1 = bf16[16,256,512]{2,1,0:T(8,128)(2,1)} async-done(((bf16[16,256,512]{2,1,0:T(8,128)(2,1)}), bf16[16,256,512]{2,1,0:T(8,128)(2,1)}, u32[]{:S(2)}, u32[]{:S(2)}) %all-to-all-start.1) | async-done | bytes 4194336 | tf_op jit(solution)/shard_map/all_to_all | solution.py:40
  109.7 12.2 %gather_fusion.1 = bf16[2048,512]{1,0:T(8,128)(2,1)} fusion(bf16[4096,512]{1,0:T(8,128)(2,1)} %bitcast.10, s32[2048]{0:T(1024)S(1)} %broadcast_clamp_fusion), kind=kCustom, calls=%fused_computation.1 | custom fusion | bytes 4202496 | tf_op jit(solution)/shard_map/jit(_take)/gather | solution.py:44
  121.9 1.9 broadcast_select_fusion
  123.8 0.9 copy-done.2
  124.7 3.0 pad_maximum_fusion.1
  127.7 10.2 %gather_fusion.2 = bf16[102,128,512]{2,1,0:T(8,128)(2,1)} fusion(bf16[48,128,512]{2,1,0:T(8,128)(2,1)} %bitcast.40, s32[1024]{0:T(1024)S(1)} %pad_clamp_fusion), kind=kCustom, calls=%fused_computation.2 | custom fusion | bytes 26739096 | tf_op jit(solution)/shard_map/jit(_take)/gather | solution.py:12
  137.9 13.8 %fusion.3 = f32[102,128,512]{1,2,0:T(8,128)} fusion(bf16[102,128,512]{2,1,0:T(8,128)(2,1)} %gather_fusion.2, pred[102]{0:T(512)(128)(4,1)S(1)} %compare_and_fusion.2, bf16[1,102,128,128]{3,2,1,0:T(8,128)(2,1)S(1)} %copy-done), kind=kOutput, calls=%fused_computation.6 | convolution fusion | flops 1717960704 | bytes 43450472 | tf_op jit(solution)/shard_map/etc,ecf->etf/dot_general | solution.py:13
  151.7 28.4 %copy.21 = f32[102,128,512]{2,0,1:T(8,128)} copy(f32[102,128,512]{1,2,0:T(8,128)} %fusion.3) | data formatting | bytes 53477376 | tf_op jit(solution)/shard_map/etc,ecf->etf/dot_general | solution.py:13
  180.1 16.6 %convolution_convert_fusion = bf16[32,128,512]{2,0,1:T(8,128)(2,1)S(1)} fusion(f32[102,128,512]{2,0,1:T(8,128)} %copy.21, f32[102]{0:T(128)S(1)} %compare_convert_fusion, s32[102]{0:T(128)S(1)} %bitcast.49), kind=kOutput, calls=%fused_computation.14 | convolution fusion | flops 2569017856 | bytes 30933808 | tf_op jit(solution)/shard_map/de,etf->dtf/dot_general | solution.py:18
  196.7 2.4 copy.22
  199.1 2.0 copy-done.5
  201.1 3.9 fusion.8
  205.3 69.3 %reduce-scatter.2.cloned.1.call-done = f32[2048,256]{1,0:T(8,128)} async-done(((f32[4096,256]{1,0:T(8,128)}), f32[2048,256]{1,0:T(8,128)}) %reduce-scatter.2.cloned.1.call-update) | async-done | bytes 2097168 | tf_op jit(solution)/shard_map/reduce_scatter | solution.py:52
  274.6 3.0 compare_select_fusion
  277.7 1.2 maximum_convert_fusion
  278.8 32.1 %all-gather.2.cloned.1.call-done = bf16[4096,256]{1,0:T(8,128)(2,1)} async-done(((bf16[2048,256]{1,0:T(8,128)(2,1)}), bf16[4096,256]{1,0:T(8,128)(2,1)}) %all-gather.2.cloned.1.call-update) | async-done | bytes 2097168 | tf_op jit(solution)/shard_map/all_gather | solution.py:61
  310.9 7.6 %fusion.7 = f32[1024,256]{1,0:T(8,128)} fusion(bf16[4096,256]{1,0:T(8,128)(2,1)} %all-gather.2.cloned.1.call-done, bf16[4096,512]{1,0:T(8,128)(2,1)} %bitcast.42, bf16[4096,512]{1,0:T(8,128)(2,1)} %param.11), kind=kOutput, calls=%fused_computation.10 | convolution fusion | flops 2164260864 | bytes 11534336 | tf_op jit(solution)/shard_map/dot_general | solution.py:63
  319.0 74.1 %all-reduce.2 = (bf16[1024,256]{1,0:T(8,128)(2,1)}, f32[256]{0:T(256)}) all-reduce(f32[1024,256]{1,0:T(8,128)} %fusion.7, f32[256]{0:T(256)S(1)} %convert_reduce_fusion), channel_id=1, replica_groups=mesh['dom'=16,'feat'=2] {'dom'}, use_global_device_ids=true, to_apply=%region_1.2 | all-reduce | flops 262400 | bytes 1574912 | tf_op jit(solution)/shard_map/psum | solution.py:68
  393.2 1.9 fusion.23
  (42 shorter events, 2.5 us)
Async XLA Ops:
  7.2 130.7 %copy-start = (bf16[1,102,128,128]{3,2,1,0:T(8,128)(2,1)S(1)}, bf16[1,102,128,128]{3,2,1,0:T(8,128)(2,1)}, u32[]{:S(2)}) copy-start(bf16[1,102,128,128]{3,2,1,0:T(8,128)(2,1)} %param.15) | copy-start | bytes 10027012
  7.2 15.4 %all-to-all-start = ((s32[1,16,128]{2,0,1:T(1,128)}), s32[1,16,128]{2,0,1:T(1,128)S(1)}, u32[]{:S(2)}, u32[]{:S(2)}) async-start(s32[1,16,128]{2,0,1:T(1,128)} %bitcast.46), calls=%async_computation | async-start | bytes 16384 | tf_op jit(solution)/shard_map/all_to_all | solution.py:41
  26.0 6.9 %copy-start.12 = (s32[1,102]{1,0:T(1,128)S(1)}, s32[1,102]{1,0:T(1,128)}, u32[]{:S(2)}) copy-start(s32[1,102]{1,0:T(1,128)} %param.17) | copy-start | bytes 1228
  26.0 83.7 %all-to-all-start.1 = ((bf16[16,256,512]{2,1,0:T(8,128)(2,1)}), bf16[16,256,512]{2,1,0:T(8,128)(2,1)}, u32[]{:S(2)}, u32[]{:S(2)}) async-start(bf16[16,256,512]{2,1,0:T(8,128)(2,1)} %stack.2), calls=%async_computation.1 | async-start | bytes 8388608 | tf_op jit(solution)/shard_map/all_to_all | solution.py:40
  32.2 242.4 %reduce-scatter.2.cloned.1.call-start = ((), (), s32[]{:S(2)}) async-start(), calls=%async_computation.3 | async-start | bytes 6291456 | tf_op jit(solution)/shard_map/reduce_scatter | solution.py:52
  121.9 2.8 copy-start.2
  151.7 28.4 %copy-start.9 = (s32[1,102]{1,0:T(1,128)S(1)}, s32[1,102]{1,0:T(1,128)}, u32[]{:S(2)}) copy-start(s32[1,102]{1,0:T(1,128)} %param.16) | copy-start | bytes 1228
  196.7 4.4 %copy-start.3 = (bf16[4096,512]{1,0:T(8,128)(2,1)S(1)}, bf16[4096,512]{1,0:T(8,128)(2,1)}, u32[]{:S(2)}) copy-start(bf16[4096,512]{1,0:T(8,128)(2,1)} %param.11) | copy-start | bytes 12582916
  196.7 4.4 %copy-start.10 = (bf16[512,256]{1,0:T(8,128)(2,1)S(1)}, bf16[512,256]{1,0:T(8,128)(2,1)}, u32[]{:S(2)}) copy-start(bf16[512,256]{1,0:T(8,128)(2,1)} %param.13) | copy-start | bytes 786436
  196.7 4.4 %copy-start.11 = (bf16[512,256]{1,0:T(8,128)(2,1)S(1)}, bf16[512,256]{1,0:T(8,128)(2,1)}, u32[]{:S(2)}) copy-start(bf16[512,256]{1,0:T(8,128)(2,1)} %param.12) | copy-start | bytes 786436
  199.1 2.0 copy-start.5
  205.0 69.6 %copy-start.7 = (bf16[2048,256]{1,0:T(8,128)(2,1)S(1)}, bf16[2048,256]{1,0:T(8,128)(2,1)}, u32[]{:S(2)}) copy-start(bf16[2048,256]{1,0:T(8,128)(2,1)} %param.21) | copy-start | bytes 3145732
  205.0 69.6 %copy-start.8 = (f32[256]{0:T(256)S(1)}, f32[256]{0:T(256)}, u32[]{:S(2)}) copy-start(f32[256]{0:T(256)} %param.14) | copy-start | bytes 3076
  205.0 105.9 %all-gather.2.cloned.1.call-start = ((), (), s32[]{:S(2)}) async-start(), calls=%async_computation.4 | async-start | bytes 3145728 | tf_op jit(solution)/shard_map/all_gather | solution.py:61
  274.6 3.1 copy-start.4
  310.9 7.6 %copy-start.6 = (bf16[4096,256]{1,0:T(8,128)(2,1)S(1)}, bf16[4096,256]{1,0:T(8,128)(2,1)}, u32[]{:S(2)}) copy-start(bf16[4096,256]{1,0:T(8,128)(2,1)} %all-gather.2.cloned.1.call-done) | copy-start | bytes 6291460
  310.9 84.1 %copy-start.1 = (bf16[1,102,128,128]{3,2,1,0:T(8,128)(2,1)S(1)}, bf16[1,102,128,128]{3,2,1,0:T(8,128)(2,1)}, u32[]{:S(2)}) copy-start(bf16[1,102,128,128]{3,2,1,0:T(8,128)(2,1)} %param.15) | copy-start | bytes 10027012
Sparse Core Ops, SparseCore 0:
  205.1 69.4 reduce-scatter.1
  277.8 33.0 all-gather.1
